TPU v7x, 32 devices: a whole 2x2x4 slice. The times are simulated.
32 devices in a mesh: ctx: 2 (over x), fsdp: 16 (over z, y, core).
Axes of the slice: x: 2, y: 2, z: 4, core: 2. Of those that a mesh axis runs over, the one named last changes fastest.
Arguments:
- hidden_in: bfloat16 [16, 256, 1280], P('fsdp', 'ctx'), may hold values from -8 to 8
- values: bfloat16 [16, 256, 2560], P('fsdp', 'ctx'), may hold values from -6 to 6
- log_decay: float32 [16, 40, 256], P('fsdp', None, 'ctx'), may hold values from -1 to 0, as said below
- doc_lengths: int32 [16, 4], P('fsdp'), may hold values from 1 to 128, 256 in all within a row
- proj_bc: bfloat16 [1280, 256], P('fsdp'), may hold values from -0.15625 to 0.15625
- grad_out: bfloat16 [16, 256, 2560], P('fsdp', 'ctx'), may hold values from -6 to 6
Outputs:
- grad_values: bfloat16 [16, 256, 2560], P('fsdp', 'ctx')
- grad_hidden: bfloat16 [16, 256, 1280], P('fsdp', 'ctx')
- grad_proj: float32 [1280, 256], P('fsdp')
Inputs may be any that keep to these rules, and one draw needn't show every extreme that they name: `doc_lengths`: each sequence's 4 document lengths sum to 256; the longest is exactly half of 256. `log_decay`: logarithms of decays, all negative.
All inputs are finite; a program needn't handle non-finite values.
Results may differ from a plain program's by a relative error of at most 0.012.
Values may be sent and summed in bfloat16 or wider, within the bound.
A program may use at most 64 MiB of HBM per device.

v0:
```python
import jax
import jax.numpy as jnp
from jax import lax
from jax.sharding import PartitionSpec as P


def entering(value, axis, combine, identity, reverse):
    length, mine = (lax.axis_size(axis), lax.axis_index(axis))
    everything = jax.tree.map(
        lambda part, kind: lax.all_gather(part.astype(kind), axis),
        value,
        (jnp.bfloat16, jnp.bfloat16),
    )
    start = jax.tree.map(
        lambda part, zero: jnp.broadcast_to(jnp.asarray(zero, part.dtype), part.shape),
        value,
        identity,
    )

    def turn(k, before):
        at = length - 1 - k if reverse else k
        reached = at > mine if reverse else at < mine
        new = combine(
            before, jax.tree.map(lambda part, own: part[at].astype(own.dtype), everything, value)
        )
        return jax.tree.map(lambda a, b: jnp.where(reached, a, b), new, before)

    return lax.fori_loop(0, length, turn, start)


def combine_pairs(first_pair, second_pair):
    first_decay, first_state = first_pair
    second_decay, second_state = second_pair
    rows_count = first_state.shape[0]
    head_count = first_decay.shape[0]
    decayed = (
        first_state.reshape(rows_count, head_count, -1) * second_decay[None, :, None]
    ).reshape(first_state.shape)
    return (first_decay * second_decay, decayed + second_state)


def block_terms(b_rows, c_rows, value_rows, grad_rows, decay_rows, doc_ids, prev_doc):
    token_count, state_size = b_rows.shape
    head_count = decay_rows.shape[0]
    inner_width = value_rows.shape[1]
    head_dim = inner_width // head_count
    cumulative = jnp.cumsum(decay_rows, axis=1)
    last_doc = doc_ids[-1]
    token_places = jnp.arange(token_count, dtype=jnp.int32)
    allowed = (doc_ids[:, None] == doc_ids[None, :]) & (
        token_places[:, None] >= token_places[None, :]
    )
    spread = cumulative[:, :, None] - cumulative[:, None, :]
    decay_matrix = jnp.where(allowed[None], jnp.exp(jnp.where(allowed[None], spread, 0.0)), 0.0)
    in_weight = jnp.exp(cumulative) * (doc_ids == prev_doc).astype(jnp.float32)[None, :]
    out_weight = (
        jnp.exp(cumulative[:, -1:] - cumulative)
        * (doc_ids == last_doc).astype(jnp.float32)[None, :]
    )
    total_decay = jnp.exp(cumulative[:, -1]) * (last_doc == prev_doc).astype(jnp.float32)
    contract_last = (((1,), (1,)), ((), ()))
    scores = (
        lax.dot_general(c_rows, b_rows, contract_last, preferred_element_type=jnp.float32)
        / state_size
    )
    mixing = (decay_matrix * scores[None]).astype(jnp.bfloat16)
    value_heads = value_rows.reshape(token_count, head_count, head_dim)
    grad_heads = grad_rows.reshape(token_count, head_count, head_dim)
    products = jnp.einsum(
        "rhp,thp->hrt", grad_heads, value_heads, preferred_element_type=jnp.float32
    )
    kernel = (jnp.sum(decay_matrix * products, axis=0) / state_size).astype(jnp.bfloat16)
    grad_value_local = jnp.einsum(
        "hrt,rhp->thp", mixing, grad_heads, preferred_element_type=jnp.float32
    ).reshape(token_count, inner_width)
    contract_first = (((0,), (0,)), ((), ()))
    grad_b_local = lax.dot_general(
        kernel, c_rows, contract_first, preferred_element_type=jnp.float32
    )
    grad_c_local = jnp.dot(kernel, b_rows, preferred_element_type=jnp.float32)
    weighted_values = (
        (out_weight.T[:, :, None] * value_heads)
        .reshape(token_count, inner_width)
        .astype(jnp.bfloat16)
    )
    weighted_grads = (
        (in_weight.T[:, :, None] * grad_heads)
        .reshape(token_count, inner_width)
        .astype(jnp.bfloat16)
    )
    local_state = lax.dot_general(
        b_rows, weighted_values, contract_first, preferred_element_type=jnp.float32
    )
    local_grad = (
        lax.dot_general(c_rows, weighted_grads, contract_first, preferred_element_type=jnp.float32)
        / state_size
    )
    return (
        total_decay,
        local_state,
        local_grad,
        out_weight,
        weighted_values,
        weighted_grads,
        grad_value_local,
        grad_b_local,
        grad_c_local,
    )


def block_finish(b_rows, terms, state_in, grad_after):
    out_weight = terms[3]
    weighted_values = terms[4]
    weighted_grads = terms[5]
    grad_value_local = terms[6]
    grad_b_local = terms[7]
    grad_c_local = terms[8]
    token_count, state_size = b_rows.shape
    head_count = out_weight.shape[0]
    inner_width = weighted_values.shape[1]
    state_used = state_in.astype(jnp.bfloat16)
    grad_used = grad_after.astype(jnp.bfloat16)
    contract_last = (((1,), (1,)), ((), ()))
    grad_c_edge = (
        lax.dot_general(
            weighted_grads, state_used, contract_last, preferred_element_type=jnp.float32
        )
        / state_size
    )
    grad_b_edge = lax.dot_general(
        weighted_values, grad_used, contract_last, preferred_element_type=jnp.float32
    )
    edge_values = jnp.dot(b_rows, grad_used, preferred_element_type=jnp.float32).reshape(
        token_count, head_count, -1
    )
    grad_value_edge = (out_weight.T[:, :, None] * edge_values).reshape(token_count, inner_width)
    grad_values = (grad_value_local + grad_value_edge).astype(jnp.bfloat16)
    grad_bc = jnp.concatenate(
        [grad_b_local + grad_b_edge, grad_c_local + grad_c_edge], axis=1
    ).astype(jnp.bfloat16)
    return (grad_values, grad_bc)


def local(hidden_in, values, log_decay, doc_lengths, proj_bc, grad_out):
    token_count = hidden_in.shape[1]
    state_size = proj_bc.shape[1] // 2
    hidden_rows = hidden_in[0]
    first_proj = lax.all_gather(proj_bc, "fsdp", axis=0, tiled=True)
    projected = jnp.dot(hidden_rows, first_proj, preferred_element_type=jnp.float32).astype(
        jnp.bfloat16
    )
    b_rows = projected[:, :state_size]
    c_rows = projected[:, state_size:]
    lengths = doc_lengths[0]
    doc_starts = jnp.cumsum(lengths) - lengths
    first_token = lax.axis_index("ctx") * token_count
    token_places = first_token + jnp.arange(token_count, dtype=jnp.int32)
    doc_ids = jnp.sum((doc_starts[None, :] <= token_places[:, None]).astype(jnp.int32), axis=1)
    prev_doc = jnp.sum((doc_starts <= first_token - 1).astype(jnp.int32))
    terms = block_terms(b_rows, c_rows, values[0], grad_out[0], log_decay[0], doc_ids, prev_doc)
    total_decay = terms[0]
    unit_pair = (jnp.ones_like(total_decay), jnp.zeros_like(terms[1]))
    state_in = entering((total_decay, terms[1]), "ctx", combine_pairs, unit_pair, False)[1]
    grad_after = entering((total_decay, terms[2]), "ctx", combine_pairs, unit_pair, True)[1]
    grad_values, grad_bc = block_finish(b_rows, terms, state_in, grad_after)
    contract_last = (((1,), (1,)), ((), ()))
    grad_hidden = lax.dot_general(
        grad_bc, first_proj, contract_last, preferred_element_type=jnp.float32
    ).astype(jnp.bfloat16)
    seq_total = lax.axis_size("fsdp") * hidden_in.shape[0]
    contract_first = (((0,), (0,)), ((), ()))
    full_term = (
        lax.dot_general(hidden_rows, grad_bc, contract_first, preferred_element_type=jnp.float32)
        / seq_total
    )
    summed = lax.psum(full_term, "ctx")
    grad_proj = lax.psum_scatter(summed, "fsdp", scatter_dimension=0, tiled=True)
    return (grad_values[None], grad_hidden[None], grad_proj)


def solution(mesh):
    in_specs = (
        P("fsdp", "ctx", None),
        P("fsdp", "ctx", None),
        P("fsdp", None, "ctx"),
        P("fsdp", None),
        P("fsdp", None),
        P("fsdp", "ctx", None),
    )
    out_specs = (P("fsdp", "ctx", None), P("fsdp", "ctx", None), P("fsdp", None))
    return jax.shard_map(local, mesh=mesh, in_specs=in_specs, out_specs=out_specs, check_vma=False)
```

profile of v0, /device:TPU:0, one launch (start us, length us, event | category | flops | bytes accessed | tf_op | source)
XLA Modules:
  0.0 186.9 jit_solution(2364739231670539729)
XLA Ops:
  9.4 1.3 fusion.33
  11.9 1.4 copy.36
  13.4 25.1 %all_gather.21 = bf16[1280,256]{1,0:T(8,128)(2,1)S(1)} all-gather(bf16[80,256]{1,0:T(8,128)(2,1)S(1)} %copy-done.8), channel_id=1, replica_groups=mesh['ctx'=2,'fsdp'=16] {'fsdp'}, dimensions={0}, use_global_device_ids=true | all-gather | bytes 696320 | tf_op jit(solution)/shard_map/all_gather | solution.py:148
  48.0 5.1 %all-reduce = bf16[80]{0:T(256)(128)(2,1)S(1)} all-reduce(bf16[80]{0:T(256)(128)(2,1)S(1)} %dynamic-update-slice), channel_id=2, replica_groups=mesh['ctx'=2,'fsdp'=16] {'ctx'}, use_global_device_ids=true, to_apply=%add | all-reduce | flops 80 | bytes 320
  53.2 2.4 %multiply_reduce_fusion = f32[128,128]{1,0:T(8,128)S(1)} fusion(bf16[128,40,64]{0,2,1:T(8,128)(2,1)} %bitcast.81, bf16[128,40,64]{0,2,1:T(8,128)(2,1)} %bitcast.83, f32[40,128]{1,0:T(8,128)S(1)} %reduce_window_sum.18, pred[128,128]{1,0:T(8,128)(4,1)S(1)} %fusion.24), kind=kOutput, calls=%fused_computation.15 | convolution fusion | flops 87146496 | bytes 1413120 | tf_op jit(solution)/shard_map/rhp,thp->hrt/dot_general | solution.py:69
  55.7 8.2 %all-gather.6.cloned.1.call-done = bf16[256,2560]{1,0:T(8,128)(2,1)} async-done(((bf16[128,2560]{1,0:T(8,128)(2,1)}), bf16[256,2560]{1,0:T(8,128)(2,1)}) %all-gather.6.cloned.1.call-update) | async-done | bytes 1310736 | tf_op jit(solution)/shard_map/all_gather | solution.py:10
  63.8 4.2 %while.30 = (s32[]{:T(128)}, f32[128,2560]{1,0:T(8,128)S(1)}, s32[]{:T(128)}, bf16[2,40]{1,0:T(2,128)(2,1)S(1)}, bf16[2,128,2560]{2,1,0:T(8,128)(2,1)}, /*index=5*/s32[]{:T(128)}, s32[]{:T(128)}, s32[]{:T(128)}) while((s32[]{:T(128)}, f32[128,2560]{1,0:T(8,128)S(1)}, s32[]{:T(128)}, bf16[2,40]{1,0:T(2,128)(2,1)S(1)}, ...), condition=%wide.region_5.6_spmd.clone, body=%wide.region_4.5_spmd.clone.sunk | while | flops 1638448 | bytes 3318319 | solution.py:28
  64.0 1.9 %fusion.51 = f32[128,2560]{1,0:T(8,128)S(1)} fusion(f32[128,2560]{1,0:T(8,128)S(1)} %get-tuple-element.374, bf16[2,128,2560]{2,1,0:T(8,128)(2,1)} %get-tuple-element.385, s32[]{:T(128)S(6)} %select_n.90, f32[2560]{0:T(1024)S(1)} %mul.207, pred[]{:T(512)S(6)} %compare.6, pred[]{:T(512)S(6)} %gt.12), kind=kLoop, calls=%fused_computation.1.clone.1 | loop fusion | flops 1638400 | bytes 3287046 | tf_op jit(solution)/shard_map/while/body/eval_jaxpr/jit(_where)/select_n | solution.py:26
  66.1 1.9 %fusion.51 = f32[128,2560]{1,0:T(8,128)S(1)} fusion(f32[128,2560]{1,0:T(8,128)S(1)} %get-tuple-element.374, bf16[2,128,2560]{2,1,0:T(8,128)(2,1)} %get-tuple-element.385, s32[]{:T(128)S(6)} %select_n.90, f32[2560]{0:T(1024)S(1)} %mul.207, pred[]{:T(512)S(6)} %compare.6, pred[]{:T(512)S(6)} %gt.12), kind=kLoop, calls=%fused_computation.1.clone.1 | loop fusion | flops 1638400 | bytes 3287046 | tf_op jit(solution)/shard_map/while/body/eval_jaxpr/jit(_where)/select_n | solution.py:26
  68.0 1.5 fusion.21
  69.5 20.1 %all-gather.8.cloned.1.call-done = bf16[256,2560]{1,0:T(8,128)(2,1)} async-done(((bf16[128,2560]{1,0:T(8,128)(2,1)}), bf16[256,2560]{1,0:T(8,128)(2,1)}) %all-gather.8.cloned.1.call-update) | async-done | bytes 1310736 | tf_op jit(solution)/shard_map/all_gather | solution.py:10
  89.6 4.2 %while.31 = (s32[]{:T(128)}, f32[128,2560]{1,0:T(8,128)S(1)}, s32[]{:T(128)}, bf16[2,40]{1,0:T(2,128)(2,1)S(1)}, bf16[2,128,2560]{2,1,0:T(8,128)(2,1)}, /*index=5*/s32[]{:T(128)}, s32[]{:T(128)}) while((s32[]{:T(128)}, f32[128,2560]{1,0:T(8,128)S(1)}, s32[]{:T(128)}, bf16[2,40]{1,0:T(2,128)(2,1)S(1)}, ...), condition=%wide.region_8.9_spmd.clone, body=%wide.region_7.8_spmd.clone.sunk | while | flops 1638444 | bytes 3318265 | solution.py:28
  89.7 1.9 %fusion.52 = f32[128,2560]{1,0:T(8,128)S(1)} fusion(f32[128,2560]{1,0:T(8,128)S(1)} %get-tuple-element.397, bf16[2,128,2560]{2,1,0:T(8,128)(2,1)} %get-tuple-element.407, s32[]{:T(128)} %get-tuple-element.396, f32[2560]{0:T(1024)S(1)} %mul.211, pred[]{:T(512)S(6)} %compare.7, pred[]{:T(512)S(6)} %lt.45), kind=kLoop, calls=%fused_computation.4.clone.1 | loop fusion | flops 1638400 | bytes 3287046 | tf_op jit(solution)/shard_map/while/body/eval_jaxpr/jit(_where)/select_n | solution.py:26
  91.8 1.9 %fusion.52 = f32[128,2560]{1,0:T(8,128)S(1)} fusion(f32[128,2560]{1,0:T(8,128)S(1)} %get-tuple-element.397, bf16[2,128,2560]{2,1,0:T(8,128)(2,1)} %get-tuple-element.407, s32[]{:T(128)} %get-tuple-element.396, f32[2560]{0:T(1024)S(1)} %mul.211, pred[]{:T(512)S(6)} %compare.7, pred[]{:T(512)S(6)} %lt.45), kind=kLoop, calls=%fused_computation.4.clone.1 | loop fusion | flops 1638400 | bytes 3287046 | tf_op jit(solution)/shard_map/while/body/eval_jaxpr/jit(_where)/select_n | solution.py:26
  93.7 1.5 convolution_multiply_fusion.4
  95.9 1.5 copy.51
  97.5 1.5 copy.38
  99.1 2.3 %fusion.8 = f32[40,128,64]{1,2,0:T(8,128)S(1)} fusion(bf16[128,40,64]{0,2,1:T(8,128)(2,1)} %bitcast.82, f32[128,128]{1,0:T(8,128)S(1)} %convolution_multiply_fusion.3, f32[40,128]{1,0:T(8,128)S(1)} %reduce_window_sum.18, pred[128,128]{1,0:T(8,128)(4,1)S(1)} %fusion.24), kind=kOutput, calls=%fused_computation.20 | convolution fusion | flops 87162880 | bytes 2068480 | tf_op jit(solution)/shard_map/hrt,rhp->thp/dot_general | solution.py:73
  101.4 1.5 copy.39
  102.9 3.0 %fusion.5 = bf16[1,128,2560]{2,1,0:T(8,128)(2,1)} fusion(f32[128,2560]{1,0:T(8,128)} %copy.39, f32[128,2560]{1,0:T(8,128)} %copy.38, f32[128,2560]{1,0:T(8,128)S(1)} %get-tuple-element.229, bf16[128,256]{1,0:T(8,128)(2,1)S(1)} %convolution_convert_fusion.2), kind=kOutput, calls=%fused_computation.12 | convolution fusion | flops 85196800 | bytes 4620288 | tf_op jit(solution)/shard_map/dot_general | solution.py:133
  105.9 50.3 %reduce-scatter.4.cloned.1.call-done = f32[80,256]{1,0:T(8,128)} async-done(((f32[1280,256]{1,0:T(8,128)}), f32[80,256]{1,0:T(8,128)}) %reduce-scatter.4.cloned.1.call-update) | async-done | bytes 81936
  156.1 1.6 copy.52
  158.9 19.9 %all-reduce.3.cloned.1.call-done = f32[80,256]{0,1:T(8,128)} async-done(((f32[80,256]{0,1:T(8,128)}), f32[80,256]{0,1:T(8,128)}) %all-reduce.3.cloned.1.call-update) | async-done | bytes 81936 | tf_op jit(solution)/shard_map/psum | solution.py:176
  178.8 1.6 copy.46
  (69 shorter events, 13.6 us)
Async XLA Ops:
  7.2 32.9 %copy-start = (bf16[1,128,1280]{2,1,0:T(8,128)(2,1)S(1)}, bf16[1,128,1280]{2,1,0:T(8,128)(2,1)}, u32[]{:S(2)}) copy-start(bf16[1,128,1280]{2,1,0:T(8,128)(2,1)} %param.10) | copy-start | bytes 983044
  7.2 6.2 %copy-start.8 = (bf16[80,256]{1,0:T(8,128)(2,1)S(1)}, bf16[80,256]{1,0:T(8,128)(2,1)}, u32[]{:S(2)}) copy-start(bf16[80,256]{1,0:T(8,128)(2,1)} %param.14) | copy-start | bytes 122884
  7.2 56.7 %all-gather.6.cloned.1.call-start = ((), (), s32[]{:S(2)}) async-start(), calls=%async_computation.1 | async-start | bytes 1966080 | tf_op jit(solution)/shard_map/all_gather | solution.py:10
  13.3 27.0 %copy-start.5 = (bf16[1,128,2560]{1,2,0:T(8,128)(2,1)}, bf16[1,128,2560]{1,2,0:T(8,128)(2,1)S(1)}, u32[]{:S(2)}) copy-start(bf16[1,128,2560]{1,2,0:T(8,128)(2,1)S(1)} %copy.36) | copy-start | bytes 1966084
  38.5 1.5 copy-start.3
  40.0 0.8 copy-start.1
  40.0 2.1 %copy-start.7 = (bf16[1,128,2560]{2,1,0:T(8,128)(2,1)S(1)}, bf16[1,128,2560]{2,1,0:T(8,128)(2,1)}, u32[]{:S(2)}) copy-start(bf16[1,128,2560]{2,1,0:T(8,128)(2,1)} %param.11) | copy-start | bytes 1966084
  42.1 47.4 %all-gather.8.cloned.1.call-start = ((), (), s32[]{:S(2)}) async-start(), calls=%async_computation.2 | async-start | bytes 1966080 | tf_op jit(solution)/shard_map/all_gather | solution.py:10
  42.5 2.3 %copy-start.6 = (bf16[1,128,2560]{1,2,0:T(8,128)(2,1)}, bf16[1,128,2560]{1,2,0:T(8,128)(2,1)S(1)}, u32[]{:S(2)}) copy-start(bf16[1,128,2560]{1,2,0:T(8,128)(2,1)S(1)} %copy.40) | copy-start | bytes 1966084
  42.6 0.9 copy-start.2
  43.6 2.9 %copy-start.9 = (u32[32]{0:T(128)S(1)}, u32[32]{0:T(128)}, u32[]{:S(2)}) copy-start(u32[32]{0:T(128)} %constant.94) | copy-start | bytes 388
  44.8 111.3 %reduce-scatter.4.cloned.1.call-start = ((), (), s32[]{:S(2)}) async-start(), calls=%async_computation.4 | async-start | bytes 1392640
  97.4 81.4 %all-reduce.3.cloned.1.call-start = ((), (), s32[]{:S(2)}) async-start(), calls=%async_computation.3 | async-start | bytes 262144 | tf_op jit(solution)/shard_map/psum | solution.py:176
  102.9 54.9 %copy-start.4 = (bf16[1280,256]{1,0:T(8,128)(2,1)S(1)}, bf16[1280,256]{1,0:T(8,128)(2,1)}, u32[]{:S(2)}) copy-start(bf16[1280,256]{1,0:T(8,128)(2,1)} %copy-done.3) | copy-start | bytes 1966084
Sparse Core Ops, SparseCore 0:
  42.2 21.5 all-gather.5
  65.4 24.1 all-gather.7
  97.5 58.5 reduce-scatter.3
  158.2 20.5 all-reduce.2
where the time goes:
time: 188 us; the launch traced here: 187 us
  waiting for transfers between devices  98.5 us (52%)
  blocking collectives  30.2 us (16%)
  between operations  16 us (9%)
  matrix products  15.2 us (8%)
  local copies, waits for them, and re-layouts  13.4 us (7%)
  other arithmetic  13.4 us (7%)
    unnamed x5, waiting for transfers between devices  50.3 us
    all_gather x2, waiting for transfers between devices, entering(): lax.all_gather(part.astype(kind), axis)  28.3 us
    all_gather x1, blocking collectives, local(): first_proj = lax.all_gather(proj_bc, 'fsdp', axis=0, tiled=True)  25.1 us
    psum x1, waiting for transfers between devices, local(): summed = lax.psum(full_term, 'ctx')  19.9 us
    unnamed x28, local copies, waits for them, and re-layouts  8.88 us
    select_n x4, other arithmetic, turn(): return jax.tree.map(lambda a, b: jnp.where(reached, a, b), new, before)  7.64 us
    unnamed x1, blocking collectives  5.12 us
  transfers between devices with their start and end apart: 4, of which 4 were waited for; matrix products, arithmetic and copies ran while one was open for 11% of the time, Pallas kernels for 0%

commit v1 on v0

--- a/solution.py
+++ b/solution.py
@@ -173,7 +173,7 @@
         lax.dot_general(hidden_rows, grad_bc, contract_first, preferred_element_type=jnp.float32)
         / seq_total
     )
-    summed = lax.psum(full_term, "ctx")
+    summed = jnp.sum(lax.all_gather(full_term, "ctx"), axis=0)
     grad_proj = lax.psum_scatter(summed, "fsdp", scatter_dimension=0, tiled=True)
     return (grad_values[None], grad_hidden[None], grad_proj)
 

time: 188 us -> 213 us (1.13)
  waiting for transfers between devices: 98.5 us -> 114 us
  other arithmetic: 13.4 us -> 18.3 us
  local copies, waits for them, and re-layouts: 13.4 us -> 16 us
    all_gather x0 -> x1, waiting for transfers between devices: none -> 38.9 us  [local(): summed = jnp.sum(lax.all_gather(full_term, 'ctx'), axis=0)]
    psum x1 -> x0, waiting for transfers between devices: 19.9 us -> none  [local(): summed = lax.psum(full_term, 'ctx')]
    reduce_sum x0 -> x1, other arithmetic: none -> 4.85 us  [local(): summed = jnp.sum(lax.all_gather(full_term, 'ctx'), axis=0)]
    all_gather x0 -> x1, local copies, waits for them, and re-layouts: none -> 4.49 us  [local(): summed = jnp.sum(lax.all_gather(full_term, 'ctx'), axis=0)]
    unnamed x5, waiting for transfers between devices: 50.3 us -> 47 us
    unnamed x28 -> x26, local copies, waits for them, and re-layouts: 8.88 us -> 5.58 us
where the time goes in v1:
time: 213 us; the launch traced here: 212 us
  waiting for transfers between devices  114 us (54%)
  blocking collectives  30.2 us (14%)
  other arithmetic  18.3 us (9%)
  matrix products  17.1 us (8%)
  local copies, waits for them, and re-layouts  16 us (8%)
  between operations  15.9 us (7%)
    unnamed x5, waiting for transfers between devices  47 us
    all_gather x1, waiting for transfers between devices, local(): summed = jnp.sum(lax.all_gather(full_term, 'ctx'), axis=0)  38.9 us
    all_gather x2, waiting for transfers between devices, entering(): lax.all_gather(part.astype(kind), axis)  28.3 us
    all_gather x1, blocking collectives, local(): first_proj = lax.all_gather(proj_bc, 'fsdp', axis=0, tiled=True)  25.1 us
    select_n x4, other arithmetic, turn(): return jax.tree.map(lambda a, b: jnp.where(reached, a, b), new, before)  7.64 us
    unnamed x26, local copies, waits for them, and re-layouts  5.58 us
    unnamed x1, blocking collectives  5.12 us
    reduce_sum x1, other arithmetic, local(): summed = jnp.sum(lax.all_gather(full_term, 'ctx'), axis=0)  4.85 us
  transfers between devices with their start and end apart: 4, of which 4 were waited for; matrix products, arithmetic and copies ran while one was open for 11% of the time, Pallas kernels for 0%

profile of v1, /device:TPU:0, one launch (start us, length us, event | category | flops | bytes accessed | tf_op | source)
XLA Modules:
  0.0 212.3 jit_solution(18342330552148218122)
XLA Ops:
  11.9 1.4 copy.45
  13.4 25.1 %all_gather.27 = bf16[1280,256]{1,0:T(8,128)(2,1)S(1)} all-gather(bf16[80,256]{1,0:T(8,128)(2,1)S(1)} %copy-done.8), channel_id=1, replica_groups=mesh['ctx'=2,'fsdp'=16] {'fsdp'}, dimensions={0}, use_global_device_ids=true | all-gather | bytes 696320 | tf_op jit(solution)/shard_map/all_gather | solution.py:148
  48.0 5.1 %all-reduce = bf16[80]{0:T(256)(128)(2,1)S(1)} all-reduce(bf16[80]{0:T(256)(128)(2,1)S(1)} %dynamic-update-slice), channel_id=2, replica_groups=mesh['ctx'=2,'fsdp'=16] {'ctx'}, use_global_device_ids=true, to_apply=%add | all-reduce | flops 80 | bytes 320
  53.2 2.4 %multiply_reduce_fusion = f32[128,128]{1,0:T(8,128)S(1)} fusion(bf16[128,40,64]{0,2,1:T(8,128)(2,1)} %bitcast.83, bf16[128,40,64]{0,2,1:T(8,128)(2,1)} %bitcast.85, f32[40,128]{1,0:T(8,128)S(1)} %reduce_window_sum.18, pred[128,128]{1,0:T(8,128)(4,1)S(1)} %fusion.24), kind=kOutput, calls=%fused_computation.15 | convolution fusion | flops 87146496 | bytes 1413120 | tf_op jit(solution)/shard_map/rhp,thp->hrt/dot_general | solution.py:69
  55.6 8.2 %all-gather.8.cloned.1.call-done = bf16[256,2560]{1,0:T(8,128)(2,1)} async-done(((bf16[128,2560]{1,0:T(8,128)(2,1)}), bf16[256,2560]{1,0:T(8,128)(2,1)}) %all-gather.8.cloned.1.call-update) | async-done | bytes 1310736 | tf_op jit(solution)/shard_map/all_gather | solution.py:10
  63.8 4.2 %while.30 = (s32[]{:T(128)}, f32[128,2560]{1,0:T(8,128)S(1)}, s32[]{:T(128)}, bf16[2,40]{1,0:T(2,128)(2,1)S(1)}, bf16[2,128,2560]{2,1,0:T(8,128)(2,1)}, /*index=5*/s32[]{:T(128)}, s32[]{:T(128)}, s32[]{:T(128)}) while((s32[]{:T(128)}, f32[128,2560]{1,0:T(8,128)S(1)}, s32[]{:T(128)}, bf16[2,40]{1,0:T(2,128)(2,1)S(1)}, ...), condition=%wide.region_5.6_spmd.clone, body=%wide.region_4.5_spmd.clone.sunk | while | flops 1638448 | bytes 3318319 | solution.py:28
  64.0 1.9 fusion.51
  66.1 1.9 fusion.51
  68.0 1.5 fusion.21
  69.5 20.1 %all-gather.10.cloned.1.call-done = bf16[256,2560]{1,0:T(8,128)(2,1)} async-done(((bf16[128,2560]{1,0:T(8,128)(2,1)}), bf16[256,2560]{1,0:T(8,128)(2,1)}) %all-gather.10.cloned.1.call-update) | async-done | bytes 1310736 | tf_op jit(solution)/shard_map/all_gather | solution.py:10
  89.6 4.2 %while.31 = (s32[]{:T(128)}, f32[128,2560]{1,0:T(8,128)S(1)}, s32[]{:T(128)}, bf16[2,40]{1,0:T(2,128)(2,1)S(1)}, bf16[2,128,2560]{2,1,0:T(8,128)(2,1)}, /*index=5*/s32[]{:T(128)}, s32[]{:T(128)}) while((s32[]{:T(128)}, f32[128,2560]{1,0:T(8,128)S(1)}, s32[]{:T(128)}, bf16[2,40]{1,0:T(2,128)(2,1)S(1)}, ...), condition=%wide.region_8.9_spmd.clone, body=%wide.region_7.8_spmd.clone.sunk | while | flops 1638444 | bytes 3318265 | solution.py:28
  89.7 1.9 fusion.52
  91.8 1.9 fusion.52
  93.7 1.5 convolution_multiply_fusion.4
  95.5 1.5 fusion.6
  97.2 38.9 %all-gather.12.cloned.1.call-done = f32[2560,256]{0,1:T(8,128)} async-done(((f32[1280,256]{0,1:T(8,128)}), f32[2560,256]{0,1:T(8,128)}) %all-gather.12.cloned.1.call-update) | async-done | bytes 2621456 | tf_op jit(solution)/shard_map/all_gather | solution.py:176
  136.1 4.5 %reshape.168 = f32[2,1280,256]{1,0,2:T(2,128)} reshape(f32[2560,256]{0,1:T(8,128)} %all-gather.12.cloned.1.call-done) | data formatting | bytes 5242880 | tf_op jit(solution)/shard_map/all_gather | solution.py:176
  140.6 4.9 %reduce_sum.39 = f32[1280,256]{0,1:T(8,128)S(1)} reduce(f32[2,1280,256]{1,0,2:T(2,128)} %reshape.168, f32[]{:T(128)} %constant.83.clone.1), dimensions={0}, to_apply=%region_9.10 | reduce | flops 327680 | bytes 3932164 | tf_op jit(solution)/shard_map/reduce_sum | solution.py:176
  145.5 1.5 copy.60
  147.1 1.5 copy.47
  148.7 3.2 %fusion.8 = f32[40,128,64]{1,2,0:T(8,128)} fusion(bf16[128,40,64]{0,2,1:T(8,128)(2,1)} %bitcast.84, f32[128,128]{1,0:T(8,128)S(1)} %convolution_multiply_fusion.3, f32[40,128]{1,0:T(8,128)S(1)} %reduce_window_sum.18, pred[128,128]{1,0:T(8,128)(4,1)S(1)} %fusion.24), kind=kOutput, calls=%fused_computation.20 | convolution fusion | flops 87162880 | bytes 2068480 | tf_op jit(solution)/shard_map/hrt,rhp->thp/dot_general | solution.py:73
  151.9 2.9 %copy.48 = f32[128,2560]{1,0:T(8,128)} copy(f32[128,2560]{0,1:T(8,128)} %bitcast.86) | data formatting | bytes 2621440 | tf_op jit(solution)/shard_map/reshape | solution.py:75
  155.8 2.9 %fusion.5 = bf16[1,128,2560]{2,1,0:T(8,128)(2,1)} fusion(f32[128,2560]{1,0:T(8,128)} %copy.48, f32[128,2560]{1,0:T(8,128)} %copy.47, f32[128,2560]{1,0:T(8,128)S(1)} %get-tuple-element.229, bf16[128,256]{1,0:T(8,128)(2,1)S(1)} %convolution_convert_fusion.2), kind=kOutput, calls=%fused_computation.12 | convolution fusion | flops 85196800 | bytes 4620288 | tf_op jit(solution)/shard_map/dot_general | solution.py:133
  158.8 47.0 %reduce-scatter.4.cloned.1.call-done = f32[80,256]{1,0:T(8,128)} async-done(((f32[1280,256]{1,0:T(8,128)}), f32[80,256]{1,0:T(8,128)}) %reduce-scatter.4.cloned.1.call-update) | async-done | bytes 81936
  (69 shorter events, 14.7 us)
Async XLA Ops:
  7.2 32.9 %copy-start = (bf16[1,128,1280]{2,1,0:T(8,128)(2,1)S(1)}, bf16[1,128,1280]{2,1,0:T(8,128)(2,1)}, u32[]{:S(2)}) copy-start(bf16[1,128,1280]{2,1,0:T(8,128)(2,1)} %param.10) | copy-start | bytes 983044
  7.2 6.2 %copy-start.8 = (bf16[80,256]{1,0:T(8,128)(2,1)S(1)}, bf16[80,256]{1,0:T(8,128)(2,1)}, u32[]{:S(2)}) copy-start(bf16[80,256]{1,0:T(8,128)(2,1)} %param.14) | copy-start | bytes 122884
  7.2 56.7 %all-gather.8.cloned.1.call-start = ((), (), s32[]{:S(2)}) async-start(), calls=%async_computation.1 | async-start | bytes 1966080 | tf_op jit(solution)/shard_map/all_gather | solution.py:10
  13.3 27.0 %copy-start.5 = (bf16[1,128,2560]{1,2,0:T(8,128)(2,1)}, bf16[1,128,2560]{1,2,0:T(8,128)(2,1)S(1)}, u32[]{:S(2)}) copy-start(bf16[1,128,2560]{1,2,0:T(8,128)(2,1)S(1)} %copy.45) | copy-start | bytes 1966084
  38.5 1.5 copy-start.3
  40.0 0.8 copy-start.1
  40.0 2.1 %copy-start.7 = (bf16[1,128,2560]{2,1,0:T(8,128)(2,1)S(1)}, bf16[1,128,2560]{2,1,0:T(8,128)(2,1)}, u32[]{:S(2)}) copy-start(bf16[1,128,2560]{2,1,0:T(8,128)(2,1)} %param.11) | copy-start | bytes 1966084
  42.1 47.4 %all-gather.10.cloned.1.call-start = ((), (), s32[]{:S(2)}) async-start(), calls=%async_computation.2 | async-start | bytes 1966080 | tf_op jit(solution)/shard_map/all_gather | solution.py:10
  42.5 2.3 %copy-start.6 = (bf16[1,128,2560]{1,2,0:T(8,128)(2,1)}, bf16[1,128,2560]{1,2,0:T(8,128)(2,1)S(1)}, u32[]{:S(2)}) copy-start(bf16[1,128,2560]{1,2,0:T(8,128)(2,1)S(1)} %copy.49) | copy-start | bytes 1966084
  42.7 0.9 copy-start.2
  43.6 2.9 %copy-start.9 = (u32[32]{0:T(128)S(1)}, u32[32]{0:T(128)}, u32[]{:S(2)}) copy-start(u32[32]{0:T(128)} %constant.94) | copy-start | bytes 388
  44.8 91.4 %all-gather.12.cloned.1.call-start = ((), (), s32[]{:S(2)}) async-start(), calls=%async_computation.3 | async-start | bytes 3932160 | tf_op jit(solution)/shard_map/all_gather | solution.py:176
  97.0 108.7 %reduce-scatter.4.cloned.1.call-start = ((), (), s32[]{:S(2)}) async-start(), calls=%async_computation.4 | async-start | bytes 1392640
  151.9 2.9 %copy-start.4 = (bf16[1280,256]{1,0:T(8,128)(2,1)S(1)}, bf16[1280,256]{1,0:T(8,128)(2,1)}, u32[]{:S(2)}) copy-start(bf16[1280,256]{1,0:T(8,128)(2,1)} %copy-done.3) | copy-start | bytes 1966084
Sparse Core Ops, SparseCore 0:
  42.2 21.5 all-gather.7
  65.4 24.1 all-gather.9
  97.1 38.9 all-gather.11
  147.1 58.5 reduce-scatter.3
